TPU v7x, 32 devices: a whole 2x2x4 slice. The times are simulated.
32 devices in a mesh: chan: 8 (over z, x), tm: 4 (over y, core).
Axes of the slice: x: 2, y: 2, z: 4, core: 2. Of those that a mesh axis runs over, the one named last changes fastest.
Arguments:
- raw_traces: bfloat16 [512, 16, 4096], P('chan', 'tm'), may hold values from -6 to 6
- owner_lists: int32 [8, 128], replicated, may hold values from -1 to 511, as said below
- source_owner: int32 [2], replicated, may hold values from 0 to 7
- source_slot: int32 [2, 8], replicated, may hold values from 0 to 31, as said below
Outputs:
- correlations: float32 [1024, 16, 256], P(('chan', 'tm'))
Inputs may be any that keep to these rules, and one draw needn't show every extreme that they name: `owner_lists`: row o lists the channels owned by owner o, live entries first and then -1; each of the 512 channels appears exactly once. A quarter of the rows hold 128 live entries, half of them 3 * 16 and a quarter 64 / 2. At most 16 live entries of one row lie in one block of 64 consecutive channels, and some row has exactly 16 in some block. `source_slot`: the 8 entries of a step are distinct and below 32, so they name live channels of that owner.
All inputs are finite; a program needn't handle non-finite values.
Results may differ from a plain program's by a relative error of at most 0.0046.
Values may be sent and summed in bfloat16 or wider, within the bound.
A program may use at most 64 MiB of HBM per device.

v0:
```python
import math
import jax
import jax.numpy as jnp
from jax import lax
from jax.sharding import PartitionSpec as P

L1 = 64
L2 = 64
L = 4096
HW = 64
LAGS = 256
STEPS = 2
EPSILON = 1e-06
TWO_PI = 2.0 * math.pi


def spread(value, axis, source):
    kept = jnp.where(lax.axis_index(axis) == source, value, 0).astype(value.dtype)
    return lax.psum(kept, axis)


def make_tables():
    sample = jnp.arange(L, dtype=jnp.int32)
    window_taper = 0.5 - 0.5 * jnp.cos(TWO_PI / L * (sample.astype(jnp.float32) + 0.5))
    inner_index = jnp.arange(L2, dtype=jnp.int32)
    first_angle = (
        TWO_PI / L2 * (inner_index[:, None] * inner_index[None, :] % L2).astype(jnp.float32)
    )
    first_table = jnp.concatenate([jnp.cos(first_angle), -jnp.sin(first_angle)], axis=1).astype(
        jnp.bfloat16
    )
    outer_index = jnp.arange(L1, dtype=jnp.int32)
    twist_angle = TWO_PI / L * (outer_index[:, None] * inner_index[None, :] % L).astype(jnp.float32)
    twist_cos = jnp.cos(twist_angle)
    twist_sin = jnp.sin(twist_angle)
    half_index = jnp.arange(L1 // 2, dtype=jnp.int32)
    second_angle = (
        TWO_PI / L1 * (outer_index[:, None] * half_index[None, :] % L1).astype(jnp.float32)
    )
    second_cos = jnp.cos(second_angle)
    second_sin = jnp.sin(second_angle)
    second_table = jnp.concatenate(
        [
            jnp.concatenate([second_cos, -second_sin], axis=1),
            jnp.concatenate([second_sin, second_cos], axis=1),
        ],
        axis=0,
    )
    span_bins = 2 * HW
    band_rows = jnp.arange(3 * span_bins, dtype=jnp.int32)
    band_cols = jnp.arange(span_bins, dtype=jnp.int32)
    band = (jnp.abs(band_rows[:, None] - span_bins - band_cols[None, :]) <= HW).astype(jnp.bfloat16)
    bin_index = jnp.arange(L // 2, dtype=jnp.int32)
    counts = (jnp.minimum(bin_index, HW) + jnp.minimum(L // 2 - 1 - bin_index, HW) + 1).astype(
        jnp.float32
    )
    lag_index = jnp.arange(LAGS, dtype=jnp.int32) - LAGS // 2
    lag_angle = TWO_PI / L * (bin_index[:, None] * lag_index[None, :] % L).astype(jnp.float32)
    weights = jnp.where(bin_index == 0, 1.0, 2.0).astype(jnp.float32)[:, None]
    inverse_table = jnp.concatenate(
        [weights * jnp.cos(lag_angle), -weights * jnp.sin(lag_angle)], axis=0
    )
    return (
        window_taper,
        first_table,
        twist_cos,
        twist_sin,
        second_table,
        band,
        counts,
        inverse_table,
    )


def whiten_block(row_block, tables):
    window_taper, first_table, twist_cos, twist_sin, second_table, band, counts = tables
    row_total = row_block.shape[0]
    half_bins = L // 2
    tapered = (
        (row_block.astype(jnp.float32) * window_taper)
        .astype(jnp.bfloat16)
        .reshape(row_total, L2, L1)
    )
    section_one = jnp.einsum(
        "nab,ak->nbk", tapered, first_table, preferred_element_type=jnp.float32
    )
    real_in = section_one[:, :, :L2]
    imag_in = section_one[:, :, L2:]
    turned = jnp.concatenate(
        [real_in * twist_cos + imag_in * twist_sin, imag_in * twist_cos - real_in * twist_sin],
        axis=1,
    )
    spectrum = jnp.einsum("ntk,tj->njk", turned, second_table, precision=lax.Precision.HIGHEST)
    real_part = spectrum[:, : L1 // 2].reshape(row_total, half_bins)
    imag_part = spectrum[:, L1 // 2 :].reshape(row_total, half_bins)
    magnitude = jnp.sqrt(real_part * real_part + imag_part * imag_part).astype(jnp.bfloat16)
    span_bins = 2 * HW
    blocks = magnitude.reshape(row_total, half_bins // span_bins, span_bins)
    padded = jnp.pad(blocks, ((0, 0), (1, 1), (0, 0)))
    joined = jnp.concatenate([padded[:, :-2], padded[:, 1:-1], padded[:, 2:]], axis=2)
    smooth = jnp.einsum("nbi,ij->nbj", joined, band, preferred_element_type=jnp.float32)
    smooth = smooth.reshape(row_total, half_bins) / counts
    denominator = smooth + EPSILON
    return jnp.concatenate([real_part / denominator, imag_part / denominator], axis=1).astype(
        jnp.bfloat16
    )


def whiten_rows(traces, tables):
    row_total = traces.shape[0]
    group_rows = math.gcd(row_total, 64)
    grouped = traces.reshape(row_total // group_rows, group_rows, traces.shape[1])
    whitened = lax.map(lambda row_block: whiten_block(row_block, tables), grouped)
    return whitened.reshape(row_total, traces.shape[1])


def correlate(own_rows, sources, inverse_table, norm_scale):
    count_rows = own_rows.shape[0]
    group_rows = math.gcd(count_rows, 8)
    half_bins = L // 2
    source_real = sources[:, :, :half_bins].astype(jnp.float32)
    source_imag = sources[:, :, half_bins:].astype(jnp.float32)

    def one_group(row_block):
        block_real = row_block[:, None, :, :half_bins].astype(jnp.float32)
        block_imag = row_block[:, None, :, half_bins:].astype(jnp.float32)
        cross_real = jnp.sum(
            block_real * source_real[None] + block_imag * source_imag[None], axis=2
        )
        cross_imag = jnp.sum(
            block_imag * source_real[None] - block_real * source_imag[None], axis=2
        )
        stacked = jnp.concatenate([cross_real, cross_imag], axis=2)
        return (
            jnp.einsum("nvk,kl->nvl", stacked, inverse_table, precision=lax.Precision.HIGHEST)
            * norm_scale
        )

    grouped = own_rows.reshape(
        count_rows // group_rows, group_rows, own_rows.shape[1], own_rows.shape[2]
    )
    result = lax.map(one_group, grouped)
    return result.reshape(count_rows, sources.shape[0], inverse_table.shape[1])


def send_plan(owner_lists, own_block, block_size, send_slots):
    source_block = jnp.floor_divide(owner_lists, block_size)
    matched = (owner_lists >= 0) & (source_block == own_block)
    ranking = jnp.cumsum(matched.astype(jnp.int32), axis=1) - 1
    offsets = owner_lists - own_block * block_size
    slot_ids = jnp.arange(send_slots, dtype=jnp.int32)
    chosen = matched[:, None, :] & (ranking[:, None, :] == slot_ids[None, :, None])
    send_rows = jnp.sum(jnp.where(chosen, offsets[:, None, :], 0), axis=2)
    send_live = jnp.any(chosen, axis=2)
    return (send_rows, send_live)


def receive_plan(owner_lists, own_block, block_size, send_slots):
    my_list = lax.dynamic_index_in_dim(owner_lists, own_block, 0, keepdims=False)
    living = my_list >= 0
    source_block = jnp.floor_divide(my_list, block_size)
    position = jnp.arange(my_list.shape[0], dtype=jnp.int32)
    earlier_same = (
        (source_block[:, None] == source_block[None, :])
        & (position[None, :] < position[:, None])
        & living[None, :]
    )
    earlier = jnp.sum(earlier_same.astype(jnp.int32), axis=1)
    receive_rows = jnp.where(living, source_block * send_slots + earlier, 0)
    return (receive_rows, living)


def pack_rows(values, send_rows, send_live):
    picked = jnp.take(values, send_rows.reshape(-1), axis=0)
    return jnp.where(send_live.reshape(-1)[:, None, None], picked, jnp.zeros((), values.dtype))


def place_rows(arrived, receive_rows, living):
    picked = jnp.take(arrived, receive_rows, axis=0)
    return jnp.where(living[:, None, None], picked, jnp.zeros((), arrived.dtype))


def body(raw_traces, owner_lists, source_owner, source_slot):
    block_size, window_count, length = raw_traces.shape
    owners = lax.axis_size("chan")
    time_shards = lax.axis_size("tm")
    capacity = owner_lists.shape[1]
    send_slots = (capacity + owners - 1) // owners
    own_block = lax.axis_index("chan")
    tables = make_tables()
    forward = tables[:7]
    inverse_table = tables[7]
    norm_scale = 1.0 / math.sqrt(window_count * time_shards * (length // 2))
    slot_share = capacity // time_shards
    send_rows, send_live = send_plan(owner_lists, own_block, block_size, send_slots)
    receive_rows, living = receive_plan(owner_lists, own_block, block_size, send_slots)
    outgoing = pack_rows(raw_traces, send_rows, send_live)
    arrived = lax.all_to_all(outgoing, "chan", split_axis=0, concat_axis=0, tiled=True)
    placed = place_rows(arrived, receive_rows, living)
    spectra = whiten_rows(placed.reshape(capacity * window_count, length), forward)
    spectra = spectra.reshape(capacity, window_count, length)
    pieces = []
    for step_index in range(STEPS):
        picked = jnp.take(spectra, source_slot[step_index], axis=0)
        sources = spread(picked, "chan", source_owner[step_index])

        def stack_term(first_row, row_count, sources=sources):
            return correlate(spectra, sources, inverse_table, norm_scale)

        pieces.append(
            lax.psum_scatter(
                stack_term(jnp.int32(0), slot_share * lax.axis_size("tm")),
                "tm",
                scatter_dimension=0,
                tiled=True,
            )
        )
    result = jnp.concatenate(pieces, axis=1)
    return result


def solution(mesh):
    return jax.shard_map(
        body,
        mesh=mesh,
        in_specs=(P("chan", "tm", None), P(), P(), P()),
        out_specs=P(("chan", "tm"), None, None),
        check_vma=False,
    )
```

profile of v0, /device:TPU:0, one launch (start us, length us, event | category | flops | bytes accessed | tf_op | source)
XLA Modules:
  0.0 586.0 jit_solution(15079302522156014081)
XLA Ops:
  9.1 7.5 %gather_fusion = bf16[128,4,4096]{2,1,0:T(4,128)(2,1)} fusion(bf16[64,4,4096]{2,1,0:T(4,128)(2,1)S(1)} %copy-done, s32[1024]{0:T(1024)S(1)} %pad_clamp_fusion.3), kind=kCustom, calls=%fused_computation.2 | custom fusion | bytes 8389120 | tf_op jit(solution)/shard_map/jit(_take)/gather | solution.py:174
  16.6 6.2 %select_select_fusion.1 = bf16[128,4,4096]{2,1,0:T(4,128)(2,1)} fusion(bf16[128,4,4096]{2,1,0:T(4,128)(2,1)} %gather_fusion, pred[128]{0:T(512)(128)(4,1)S(1)} %compare_and_fusion.4, pred[128]{0:T(512)(128)(4,1)S(1)} %broadcast_in_dim.142), kind=kLoop, calls=%fused_computation.94 | loop fusion | flops 4194304 | bytes 8388864 | tf_op jit(solution)/shard_map/jit(_where)/select_n | solution.py:175
  22.8 7.4 %all-to-all-start = ((bf16[128,4,4096]{2,1,0:T(4,128)(2,1)}), bf16[128,4,4096]{2,1,0:T(4,128)(2,1)}, u32[]{:S(2)}, u32[]{:S(2)}) async-start(bf16[128,4,4096]{2,1,0:T(4,128)(2,1)} %select_select_fusion.1), calls=%async_computation | async-start | bytes 8388608 | tf_op jit(solution)/shard_map/all_to_all | solution.py:198
  35.3 9.6 %cosine_multiply_fusion = (f32[2048,256]{1,0:T(8,128)}, f32[2048,256]{1,0:T(8,128)}) fusion(s32[256]{0:T(256)S(1)} %iota_add_fusion.1, f32[2048]{0:T(1024)S(1)} %get-tuple-element.347, f32[2048]{0:T(1024)S(1)} %get-tuple-element.348), kind=kLoop, calls=%fused_computation.102 | loop fusion | flops 8388608 | bytes 4211712 | tf_op jit(solution)/shard_map/mul | solution.py:61
  44.9 78.6 %all-to-all-done = bf16[128,4,4096]{2,1,0:T(4,128)(2,1)} async-done(((bf16[128,4,4096]{2,1,0:T(4,128)(2,1)}), bf16[128,4,4096]{2,1,0:T(4,128)(2,1)}, u32[]{:S(2)}, u32[]{:S(2)}) %all-to-all-start) | async-done | bytes 4194336 | tf_op jit(solution)/shard_map/all_to_all | solution.py:198
  123.5 9.7 %gather_fusion.1 = bf16[128,4,4096]{2,1,0:T(4,128)(2,1)} fusion(bf16[128,4,4096]{2,1,0:T(4,128)(2,1)} %all-to-all-done, s32[1024]{0:T(1024)S(1)} %pad_clamp_fusion.2), kind=kCustom, calls=%fused_computation.3 | custom fusion | bytes 8389120 | tf_op jit(solution)/shard_map/jit(_take)/gather | solution.py:179
  133.2 6.9 %gather.15 = bf16[8,64,4096]{2,1,0:T(8,128)(2,1)} reshape(bf16[128,4,4096]{2,1,0:T(4,128)(2,1)} %gather_fusion.1) | data formatting | bytes 8388608 | tf_op jit(solution)/shard_map/jit(_take)/gather | solution.py:179
  140.1 3.9 select_select_fusion
  144.0 111.5 %while.39 = (s32[]{:T(128)}, bf16[8,64,4096]{2,1,0:T(8,128)(2,1)}, bf16[8,64,4096]{2,1,0:T(8,128)(2,1)}, bf16[64,128]{1,0:T(8,128)(2,1)S(1)}, f32[128,64]{0,1:T(8,128)S(1)}, /*index=5*/s32[384]{0:T(512)S(1)}) while((s32[]{:T(128)}, bf16[8,64,4096]{2,1,0:T(8,128)(2,1)}, bf16[8,64,4096]{2,1,0:T(8,128)(2,1)}, ...), condition=%wide.region_5.6_spmd.clone.clone.clone, body=%wide.region_4.5_spmd.clone.clone.sunk.clone | while | flops 578314240 | bytes 28805220 | solution.py:113
  148.0 2.0 fusion.169
  150.9 2.6 fusion.171
  162.0 2.0 fusion.169
  164.8 2.6 fusion.171
  175.9 2.0 fusion.169
  178.8 2.6 fusion.171
  189.9 2.0 fusion.169
  192.7 2.6 fusion.171
  203.8 2.0 fusion.169
  206.7 2.6 fusion.171
  217.7 2.0 fusion.169
  220.6 2.6 fusion.171
  234.5 2.6 fusion.171
  248.4 2.6 fusion.171
  255.4 7.2 %reshape_reshape.4 = bf16[128,4,4096]{2,1,0:T(4,128)(2,1)} reshape(bf16[8,64,4096]{2,1,0:T(8,128)(2,1)} %get-tuple-element.201) | data formatting | bytes 8388608 | tf_op jit(solution)/shard_map/reshape;reshape | solution.py:201
  262.6 3.1 gather_fusion.3
  265.7 3.0 gather_fusion.2
  270.6 3.8 pad_maximum_fusion
  274.4 7.3 %reshape_reshape_reshape.4 = bf16[16,8,4,4096]{3,2,1,0:T(4,128)(2,1)} reshape(bf16[8,64,4096]{2,1,0:T(8,128)(2,1)} %get-tuple-element.201) | data formatting | bytes 8388608 | tf_op jit(solution)/shard_map/reshape;reshape;reshape | solution.py:139
  281.7 61.0 %all-reduce.4.cloned.1.call-done = (bf16[8,4,4096]{2,1,0:T(4,128)(2,1)}, bf16[8,4,4096]{2,1,0:T(4,128)(2,1)}) async-done(((bf16[8,4,4096]{2,1,0:T(4,128)(2,1)}, bf16[8,4,4096]{2,1,0:T(4,128)(2,1)}), (bf16[8,4,4096]{2,1,0:T(4,128)(2,1)}, bf16[8,4,4096]{2,1,0:T(4,128)(2,1)})) %all-reduce.4.cloned.1.call-update) | async-done | bytes 524304 | tf_op jit(solution)/shard_map/psum | solution.py:19
  344.2 98.0 %while.37 = (s32[]{:T(128)}, f32[16,8,8,256]{3,2,1,0:T(8,128)S(1)}, bf16[16,8,4,4096]{3,2,1,0:T(4,128)(2,1)}, f32[8,4,2048]{2,0,1:T(8,128)S(1)}, f32[8,4,2048]{2,0,1:T(8,128)S(1)}, /*index=5*/f32[4096,256]{1,0:T(8,128)}) while((s32[]{:T(128)}, f32[16,8,8,256]{3,2,1,0:T(8,128)S(1)}, bf16[16,8,4,4096]{3,2,1,0:T(4,128)(2,1)}, ...), condition=%wide.region_10.12_spmd.clone, body=%wide.region_7.11_spmd.sunk.clone | while | flops 809648128 | bytes 8716365 | solution.py:142
  345.9 4.4 fusion.160
  352.0 4.4 fusion.160
  358.1 4.4 fusion.160
  364.2 4.4 fusion.160
  370.3 4.4 fusion.160
  376.5 4.4 fusion.160
  382.6 4.4 fusion.160
  388.7 4.4 fusion.160
  394.8 4.4 fusion.160
  400.9 4.4 fusion.160
  407.1 4.4 fusion.160
  413.2 4.4 fusion.160
  419.3 4.4 fusion.160
  425.4 4.4 fusion.160
  431.6 4.4 fusion.160
  437.7 4.4 fusion.160
  445.7 107.7 %while.38 = (s32[]{:T(128)}, f32[16,8,8,256]{3,2,1,0:T(8,128)}, bf16[16,8,4,4096]{3,2,1,0:T(4,128)(2,1)}, f32[8,4,2048]{2,0,1:T(8,128)S(1)}, f32[8,4,2048]{2,0,1:T(8,128)S(1)}, /*index=5*/f32[4096,256]{1,0:T(8,128)}) while((s32[]{:T(128)}, f32[16,8,8,256]{3,2,1,0:T(8,128)}, bf16[16,8,4,4096]{3,2,1,0:T(4,128)(2,1)}, ...), condition=%wide.region_16.18_spmd.clone, body=%wide.region_13.17_spmd.sunk.clone | while | flops 809648128 | bytes 8716873 | solution.py:142
  447.3 5.1 fusion.163
  454.2 5.1 fusion.163
  460.9 5.1 fusion.163
  467.6 5.1 fusion.163
  474.4 5.1 fusion.163
  481.1 5.1 fusion.163
  487.8 5.1 fusion.163
  494.5 5.1 fusion.163
  501.3 5.1 fusion.163
  508.0 5.1 fusion.163
  514.7 5.1 fusion.163
  521.4 5.1 fusion.163
  528.2 5.1 fusion.163
  534.9 5.1 fusion.163
  541.6 5.1 fusion.163
  548.4 5.1 fusion.163
  553.5 24.1 %reduce-scatter.5.cloned.1.call-done = f32[32,8,256]{2,1,0:T(8,128)} async-done(((f32[128,8,256]{2,1,0:T(8,128)}), f32[32,8,256]{2,1,0:T(8,128)}) %reduce-scatter.5.cloned.1.call-update) | async-done | bytes 262160 | tf_op jit(solution)/shard_map/reduce_scatter | solution.py:211
  (320 shorter events, 145.7 us)
Async XLA Ops:
  6.5 2.6 copy-start
  22.8 10.1 %copy-start.5 = (s32[2]{0:T(128)S(1)}, s32[2]{0:T(128)}, u32[]{:S(2)}) copy-start(s32[2]{0:T(128)} %param.14) | copy-start | bytes 28
  22.8 11.9 %copy-start.6 = (s32[2,8]{1,0:T(2,128)S(1)}, s32[2,8]{1,0:T(2,128)}, u32[]{:S(2)}) copy-start(s32[2,8]{1,0:T(2,128)} %param.15) | copy-start | bytes 196
  22.8 100.7 %all-to-all-start = ((bf16[128,4,4096]{2,1,0:T(4,128)(2,1)}), bf16[128,4,4096]{2,1,0:T(4,128)(2,1)}, u32[]{:S(2)}, u32[]{:S(2)}) async-start(bf16[128,4,4096]{2,1,0:T(4,128)(2,1)} %select_select_fusion.1), calls=%async_computation | async-start | bytes 8388608 | tf_op jit(solution)/shard_map/all_to_all | solution.py:198
  30.2 312.5 %all-reduce.4.cloned.1.call-start = ((), (), s32[]{:S(2)}) async-start(), calls=%async_computation.5 | async-start | bytes 1048576 | tf_op jit(solution)/shard_map/psum | solution.py:19
  154.8 1.2 copy-start.2
  168.8 1.2 copy-start.2
  182.8 1.2 copy-start.2
  196.7 1.2 copy-start.2
  210.6 1.2 copy-start.2
  224.5 1.2 copy-start.2
  238.4 1.2 copy-start.2
  252.4 1.2 copy-start.2
  262.6 8.0 %copy-start.3 = (f32[2048,256]{1,0:T(8,128)S(1)}, f32[2048,256]{1,0:T(8,128)}, u32[]{:S(2)}) copy-start(f32[2048,256]{1,0:T(8,128)} %get-tuple-element.333) | copy-start | bytes 6291460
  270.5 282.9 %reduce-scatter.3.cloned.1.call-start = ((), (), s32[]{:S(2)}) async-start(), calls=%async_computation.3 | async-start | bytes 1310720 | tf_op jit(solution)/shard_map/reduce_scatter | solution.py:211
  442.1 1.1 copy-start.4
  443.2 134.4 %reduce-scatter.5.cloned.1.call-start = ((), (), s32[]{:S(2)}) async-start(), calls=%async_computation.4 | async-start | bytes 1310720 | tf_op jit(solution)/shard_map/reduce_scatter | solution.py:211
  553.4 26.0 %copy-start.1 = (bf16[64,4,4096]{2,1,0:T(4,128)(2,1)S(1)}, bf16[64,4,4096]{2,1,0:T(4,128)(2,1)}, u32[]{:S(2)}) copy-start(bf16[64,4,4096]{2,1,0:T(4,128)(2,1)} %param.12) | copy-start | bytes 6291460
Sparse Core Ops, SparseCore 0:
  270.6 72.0 all-reduce.3
  443.3 23.9 reduce-scatter.2
  553.6 23.9 reduce-scatter.4
where the time goes:
time: 590 us; the launch traced here: 586 us
  matrix products  193 us (33%)
  waiting for transfers between devices  164 us (28%)
  local copies, waits for them, and re-layouts  119 us (20%)
  other arithmetic  87.6 us (15%)
  between operations  14.6 us (2%)
  starting transfers between devices  7.53 us (1%)
    dot_general x32, matrix products, one_group(): jnp.einsum('nvk,kl->nvl', stacked, inverse_table, precision=lax.Precision...  152 us
    all_to_all x1, waiting for transfers between devices, body(): lax.all_to_all(outgoing, 'chan', split_axis=0, concat_axis=0, tiled=True)  78.6 us
    psum x1, waiting for transfers between devices, spread(): return lax.psum(kept, axis)  61 us
    squeeze x32, local copies, waits for them, and re-layouts, correlate(): result = lax.map(one_group, grouped)  33.4 us
    reduce_scatter x2, waiting for transfers between devices, body(): lax.psum_scatter(stack_term(jnp.int32(0), slot_share * lax.axis_size('tm'...  24.1 us
    convert_element_type x16, local copies, waits for them, and re-layouts, whiten_block(): row_block.astype(jnp.float32) * window_taper  21.4 us
    dot_general x8, matrix products, whiten_block(): jnp.einsum('ntk,tj->njk', turned, second_table, precision=lax.Precision.H...  20.9 us
    reduce_sum x32, other arithmetic, one_group(): jnp.sum(block_real * source_real[None] + block_imag * source_imag[None],...  18.1 us
  transfers between devices with their start and end apart: 4, of which 3 were waited for; matrix products, arithmetic and copies ran while one was open for 23% of the time, Pallas kernels for 0%

commit v1 on v0

--- a/solution.py
+++ b/solution.py
@@ -14,9 +14,13 @@
 TWO_PI = 2.0 * math.pi
 
 
+def _store_set(page, net_axis):
+    return lax.all_gather(page, net_axis).sum(axis=0)
+
+
 def spread(value, axis, source):
     kept = jnp.where(lax.axis_index(axis) == source, value, 0).astype(value.dtype)
-    return lax.psum(kept, axis)
+    return _store_set(kept, axis)
 
 
 def make_tables():

time: 590 us -> 566 us (0.959)
  waiting for transfers between devices: 164 us -> 138 us
    psum x1 -> x0, waiting for transfers between devices: 61 us -> none  [spread(): return lax.psum(kept, axis)]
    all_gather x0 -> x2, waiting for transfers between devices: none -> 25.6 us  [_store_set(): return lax.all_gather(page, net_axis).sum(axis=0)]
    all_to_all x1, waiting for transfers between devices: 78.6 us -> 88.8 us  [body(): lax.all_to_all(outgoing, 'chan', split_axis=0, concat_axis=0, tiled=True)]
  transfers between devices with their start and end apart: 4 -> 5, of which waited for: 3 -> 3; matrix products, arithmetic and copies ran while one was open for 23% -> 42% of each run, Pallas kernels for 0% -> 0%
where the time goes in v1:
time: 566 us; the launch traced here: 562 us
  matrix products  193 us (34%)
  waiting for transfers between devices  138 us (24%)
  local copies, waits for them, and re-layouts  118 us (21%)
  other arithmetic  88.4 us (16%)
  between operations  14.5 us (3%)
  starting transfers between devices  8.24 us (1%)
    dot_general x32, matrix products, one_group(): jnp.einsum('nvk,kl->nvl', stacked, inverse_table, precision=lax.Precision...  152 us
    all_to_all x1, waiting for transfers between devices, body(): lax.all_to_all(outgoing, 'chan', split_axis=0, concat_axis=0, tiled=True)  88.8 us
    squeeze x32, local copies, waits for them, and re-layouts, correlate(): result = lax.map(one_group, grouped)  33.4 us
    all_gather x2, waiting for transfers between devices, _store_set(): return lax.all_gather(page, net_axis).sum(axis=0)  25.6 us
    reduce_scatter x2, waiting for transfers between devices, body(): lax.psum_scatter(stack_term(jnp.int32(0), slot_share * lax.axis_size('tm'...  23.7 us
    convert_element_type x16, local copies, waits for them, and re-layouts, whiten_block(): row_block.astype(jnp.float32) * window_taper  21.5 us
    dot_general x8, matrix products, whiten_block(): jnp.einsum('ntk,tj->njk', turned, second_table, precision=lax.Precision.H...  20.9 us
    reduce_sum x32, other arithmetic, one_group(): jnp.sum(block_real * source_real[None] + block_imag * source_imag[None],...  18.1 us
  transfers between devices with their start and end apart: 5, of which 3 were waited for; matrix products, arithmetic and copies ran while one was open for 42% of the time, Pallas kernels for 0%

profile of v1, /device:TPU:0, one launch (start us, length us, event | category | flops | bytes accessed | tf_op | source)
XLA Modules:
  0.0 561.7 jit_solution(10236998391691495366)
XLA Ops:
  9.1 7.5 %gather_fusion = bf16[128,4,4096]{2,1,0:T(4,128)(2,1)} fusion(bf16[64,4,4096]{2,1,0:T(4,128)(2,1)S(1)} %copy-done, s32[1024]{0:T(1024)S(1)} %pad_clamp_fusion.3), kind=kCustom, calls=%fused_computation.2 | custom fusion | bytes 8389120 | tf_op jit(solution)/shard_map/jit(_take)/gather | solution.py:178
  16.6 6.2 %select_select_fusion.1 = bf16[128,4,4096]{2,1,0:T(4,128)(2,1)} fusion(bf16[128,4,4096]{2,1,0:T(4,128)(2,1)} %gather_fusion, pred[128]{0:T(512)(128)(4,1)S(1)} %compare_and_fusion.4, pred[128]{0:T(512)(128)(4,1)S(1)} %broadcast_in_dim.142), kind=kLoop, calls=%fused_computation.94 | loop fusion | flops 4194304 | bytes 8388864 | tf_op jit(solution)/shard_map/jit(_where)/select_n | solution.py:179
  22.8 7.4 %all-to-all-start = ((bf16[128,4,4096]{2,1,0:T(4,128)(2,1)}), bf16[128,4,4096]{2,1,0:T(4,128)(2,1)}, u32[]{:S(2)}, u32[]{:S(2)}) async-start(bf16[128,4,4096]{2,1,0:T(4,128)(2,1)} %select_select_fusion.1), calls=%async_computation | async-start | bytes 8388608 | tf_op jit(solution)/shard_map/all_to_all | solution.py:202
  34.7 88.8 %all-to-all-done = bf16[128,4,4096]{2,1,0:T(4,128)(2,1)} async-done(((bf16[128,4,4096]{2,1,0:T(4,128)(2,1)}), bf16[128,4,4096]{2,1,0:T(4,128)(2,1)}, u32[]{:S(2)}, u32[]{:S(2)}) %all-to-all-start) | async-done | bytes 4194336 | tf_op jit(solution)/shard_map/all_to_all | solution.py:202
  123.5 9.7 %gather_fusion.1 = bf16[128,4,4096]{2,1,0:T(4,128)(2,1)} fusion(bf16[128,4,4096]{2,1,0:T(4,128)(2,1)} %all-to-all-done, s32[1024]{0:T(1024)S(1)} %pad_clamp_fusion.2), kind=kCustom, calls=%fused_computation.3 | custom fusion | bytes 8389120 | tf_op jit(solution)/shard_map/jit(_take)/gather | solution.py:183
  133.2 6.9 %gather.15 = bf16[8,64,4096]{2,1,0:T(8,128)(2,1)} reshape(bf16[128,4,4096]{2,1,0:T(4,128)(2,1)} %gather_fusion.1) | data formatting | bytes 8388608 | tf_op jit(solution)/shard_map/jit(_take)/gather | solution.py:183
  140.1 3.9 select_select_fusion
  144.0 111.6 %while.39 = (s32[]{:T(128)}, bf16[8,64,4096]{2,1,0:T(8,128)(2,1)}, bf16[8,64,4096]{2,1,0:T(8,128)(2,1)}, bf16[64,128]{1,0:T(8,128)(2,1)S(1)}, f32[128,64]{0,1:T(8,128)S(1)}, /*index=5*/s32[384]{0:T(512)S(1)}) while((s32[]{:T(128)}, bf16[8,64,4096]{2,1,0:T(8,128)(2,1)}, bf16[8,64,4096]{2,1,0:T(8,128)(2,1)}, ...), condition=%wide.region_5.6_spmd.clone.clone.clone, body=%wide.region_4.5_spmd.clone.clone.sunk.clone | while | flops 578314240 | bytes 28805220 | solution.py:117
  148.0 2.0 fusion.169
  150.9 2.6 fusion.171
  162.0 2.0 fusion.169
  164.8 2.6 fusion.171
  175.9 2.0 fusion.169
  178.8 2.6 fusion.171
  192.7 2.6 fusion.171
  203.8 2.0 fusion.169
  206.7 2.6 fusion.171
  220.6 2.6 fusion.171
  234.6 2.6 fusion.171
  248.5 2.6 fusion.171
  255.5 7.2 %reshape_reshape.4 = bf16[128,4,4096]{2,1,0:T(4,128)(2,1)} reshape(bf16[8,64,4096]{2,1,0:T(8,128)(2,1)} %get-tuple-element.201) | data formatting | bytes 8388608 | tf_op jit(solution)/shard_map/reshape;reshape | solution.py:205
  262.7 3.0 gather_fusion.2
  267.5 8.3 %cosine_multiply_fusion = (f32[2048,256]{1,0:T(8,128)S(1)}, f32[2048,256]{1,0:T(8,128)S(1)}) fusion(s32[256]{0:T(256)S(1)} %iota_add_fusion.1, f32[2048]{0:T(1024)S(1)} %get-tuple-element.343, f32[2048]{0:T(1024)S(1)} %get-tuple-element.344), kind=kLoop, calls=%fused_computation.102 | loop fusion | flops 8388608 | bytes 4211712 | tf_op jit(solution)/shard_map/mul | solution.py:65
  275.7 2.2 pad_maximum_fusion
  278.0 7.2 %reshape_reshape_reshape.4 = bf16[16,8,4,4096]{3,2,1,0:T(4,128)(2,1)} reshape(bf16[8,64,4096]{2,1,0:T(8,128)(2,1)} %get-tuple-element.201) | data formatting | bytes 8388608 | tf_op jit(solution)/shard_map/reshape;reshape;reshape | solution.py:143
  285.2 3.0 gather_fusion.3
  289.4 25.6 %all-gather.5.cloned.1.call-done = bf16[64,4,4096]{2,1,0:T(4,128)(2,1)} async-done(((bf16[8,4,4096]{2,1,0:T(4,128)(2,1)}), bf16[64,4,4096]{2,1,0:T(4,128)(2,1)}) %all-gather.5.cloned.1.call-update) | async-done | bytes 2097168 | tf_op jit(solution)/shard_map/all_gather | solution.py:18
  315.0 2.8 reduce_sum.86
  318.3 98.0 %while.37 = (s32[]{:T(128)}, f32[16,8,8,256]{3,2,1,0:T(8,128)S(1)}, bf16[16,8,4,4096]{3,2,1,0:T(4,128)(2,1)}, f32[8,4,2048]{2,0,1:T(8,128)S(1)}, f32[8,4,2048]{2,0,1:T(8,128)S(1)}, /*index=5*/f32[4096,256]{1,0:T(8,128)}) while((s32[]{:T(128)}, f32[16,8,8,256]{3,2,1,0:T(8,128)S(1)}, bf16[16,8,4,4096]{3,2,1,0:T(4,128)(2,1)}, ...), condition=%wide.region_10.12_spmd.clone, body=%wide.region_7.11_spmd.sunk.clone | while | flops 809648128 | bytes 8716365 | solution.py:146
  320.0 4.4 fusion.160
  326.1 4.4 fusion.160
  332.2 4.5 fusion.160
  338.3 4.4 fusion.160
  344.5 4.4 fusion.160
  350.6 4.5 fusion.160
  356.7 4.4 fusion.160
  362.9 4.4 fusion.160
  369.0 4.4 fusion.160
  375.1 4.4 fusion.160
  381.2 4.4 fusion.160
  387.4 4.4 fusion.160
  393.5 4.4 fusion.160
  399.6 4.4 fusion.160
  405.7 4.4 fusion.160
  411.8 4.4 fusion.160
  417.4 2.8 reduce_sum.87
  421.7 107.8 %while.38 = (s32[]{:T(128)}, f32[16,8,8,256]{3,2,1,0:T(8,128)}, bf16[16,8,4,4096]{3,2,1,0:T(4,128)(2,1)}, f32[8,4,2048]{2,0,1:T(8,128)S(1)}, f32[8,4,2048]{2,0,1:T(8,128)S(1)}, /*index=5*/f32[4096,256]{1,0:T(8,128)}) while((s32[]{:T(128)}, f32[16,8,8,256]{3,2,1,0:T(8,128)}, bf16[16,8,4,4096]{3,2,1,0:T(4,128)(2,1)}, ...), condition=%wide.region_16.18_spmd.clone, body=%wide.region_13.17_spmd.sunk.clone | while | flops 809648128 | bytes 8716873 | solution.py:146
  423.4 5.2 fusion.163
  430.2 5.1 fusion.163
  437.0 5.1 fusion.163
  443.7 5.1 fusion.163
  450.5 5.1 fusion.163
  457.2 5.1 fusion.163
  463.9 5.1 fusion.163
  470.6 5.1 fusion.163
  477.4 5.1 fusion.163
  484.1 5.1 fusion.163
  490.8 5.1 fusion.163
  497.6 5.1 fusion.163
  504.3 5.1 fusion.163
  511.0 5.1 fusion.163
  517.7 5.1 fusion.163
  524.5 5.1 fusion.163
  529.6 23.7 %reduce-scatter.5.cloned.1.call-done = f32[32,8,256]{2,1,0:T(8,128)} async-done(((f32[128,8,256]{2,1,0:T(8,128)}), f32[32,8,256]{2,1,0:T(8,128)}) %reduce-scatter.5.cloned.1.call-update) | async-done | bytes 262160 | tf_op jit(solution)/shard_map/reduce_scatter | solution.py:215
  (324 shorter events, 148.5 us)
Async XLA Ops:
  6.5 2.6 copy-start
  22.8 10.2 %copy-start.4 = (s32[2]{0:T(128)S(1)}, s32[2]{0:T(128)}, u32[]{:S(2)}) copy-start(s32[2]{0:T(128)} %param.14) | copy-start | bytes 28
  22.8 11.3 %copy-start.5 = (s32[2,8]{1,0:T(2,128)S(1)}, s32[2,8]{1,0:T(2,128)}, u32[]{:S(2)}) copy-start(s32[2,8]{1,0:T(2,128)} %param.15) | copy-start | bytes 196
  22.8 100.7 %all-to-all-start = ((bf16[128,4,4096]{2,1,0:T(4,128)(2,1)}), bf16[128,4,4096]{2,1,0:T(4,128)(2,1)}, u32[]{:S(2)}, u32[]{:S(2)}) async-start(bf16[128,4,4096]{2,1,0:T(4,128)(2,1)} %select_select_fusion.1), calls=%async_computation | async-start | bytes 8388608 | tf_op jit(solution)/shard_map/all_to_all | solution.py:202
  30.2 284.8 %all-gather.5.cloned.1.call-start = ((), (), s32[]{:S(2)}) async-start(), calls=%async_computation.5 | async-start | bytes 2359296 | tf_op jit(solution)/shard_map/all_gather | solution.py:18
  154.8 1.2 copy-start.2
  168.8 1.2 copy-start.2
  182.8 1.2 copy-start.2
  196.7 1.2 copy-start.2
  210.6 1.2 copy-start.2
  224.6 1.2 copy-start.2
  238.5 1.2 copy-start.2
  252.5 1.2 copy-start.2
  266.6 150.7 %all-gather.7.cloned.1.call-start = ((), (), s32[]{:S(2)}) async-start(), calls=%async_computation.6 | async-start | bytes 2359296 | tf_op jit(solution)/shard_map/all_gather | solution.py:18
  289.1 240.5 %reduce-scatter.3.cloned.1.call-start = ((), (), s32[]{:S(2)}) async-start(), calls=%async_computation.3 | async-start | bytes 1310720 | tf_op jit(solution)/shard_map/reduce_scatter | solution.py:215
  416.3 1.0 copy-start.3
  417.3 136.0 %reduce-scatter.5.cloned.1.call-start = ((), (), s32[]{:S(2)}) async-start(), calls=%async_computation.4 | async-start | bytes 1310720 | tf_op jit(solution)/shard_map/reduce_scatter | solution.py:215
  529.5 25.6 %copy-start.1 = (bf16[64,4,4096]{2,1,0:T(4,128)(2,1)S(1)}, bf16[64,4,4096]{2,1,0:T(4,128)(2,1)}, u32[]{:S(2)}) copy-start(bf16[64,4,4096]{2,1,0:T(4,128)(2,1)} %param.12) | copy-start | bytes 6291460
Sparse Core Ops, SparseCore 0:
  266.7 48.2 all-gather.4
  317.1 47.6 all-gather.6
  417.4 23.6 reduce-scatter.2
  529.7 23.5 reduce-scatter.4
